TPU v7x, 32 devices: a whole 2x2x4 slice. The times are simulated.
32 devices in a mesh: dp: 8 (over y, x, core), tensor: 4 (over z).
Axes of the slice: x: 2, y: 2, z: 4, core: 2. Of those that a mesh axis runs over, the one named last changes fastest.
Arguments:
- hidden: bfloat16 [8192, 1536], P('dp'), may hold values from -6 to 6
- norm_gain: float32 [1536], replicated, may hold values from 0.25 to 1.75
- zx_proj: bfloat16 [1536, 2, 3072], P(None, None, 'tensor'), may hold values from -0.15625 to 0.15625
- bc_proj: bfloat16 [1536, 256], replicated, may hold values from -0.15625 to 0.15625
- dt_proj: bfloat16 [1536, 48], P(None, 'tensor'), may hold values from -0.15625 to 0.15625
- conv_x: float32 [5, 3072], P(None, 'tensor'), may hold values from -3 to 3
- conv_bc: float32 [5, 256], replicated, may hold values from -3 to 3
- dt_bias: float32 [48], P('tensor'), may hold values from -7 to -3
- a_log: float32 [48], P('tensor'), may hold values from -4 to 0.5
- d_skip: float32 [48], P('tensor'), may hold values from 0.5 to 1.5
- gate_gain: float32 [3072], P('tensor'), may hold values from 0.25 to 1.75
- out_proj: bfloat16 [1536, 3072], P(None, 'tensor'), may hold values from -0.109375 to 0.109375
- cotangent: bfloat16 [8192, 1536], P('dp'), may hold values from -6 to 6
Outputs:
- block_out: bfloat16 [8192, 1536], P('dp')
- grad_hidden: bfloat16 [8192, 1536], P('dp')
- grad_norm_gain: float32 [1536], replicated
- grad_zx_proj: float32 [1536, 2, 3072], P('dp', None, 'tensor')
- grad_bc_proj: float32 [1536, 256], P('dp')
- grad_dt_proj: float32 [1536, 48], P('dp', 'tensor')
- grad_conv_x: float32 [5, 3072], P(None, 'tensor')
- grad_conv_bc: float32 [5, 256], replicated
- grad_dt_bias: float32 [48], P('tensor')
- grad_a_log: float32 [48], P('tensor')
- grad_d_skip: float32 [48], P('tensor')
- grad_gate_gain: float32 [3072], P('tensor')
- grad_out_proj: float32 [1536, 3072], P('dp', 'tensor')
All inputs are finite; a program needn't handle non-finite values.
Results may differ from a plain program's by a relative error of at most 0.005.
The roundings to bfloat16 on the way count: a program that leaves them out, or rounds other values in their place, can miss the bound.
Values may be sent and summed in bfloat16 or wider, within the bound.
No kernel may reach another device: no remote copies, remote signals or barrier semaphores. Data moves between devices by JAX's collectives and lax.ppermute only.
A program may use at most 192 MiB of HBM per device.

v0:
```python
import jax
import jax.numpy as jnp
from jax import lax
from jax.sharding import PartitionSpec as P

KCONV = 4
BLOCK_LEN = 256
SEQ_DEVS = 8
EPSILON = 1e-05
PRECISE = lax.Precision.HIGHEST


def shifted(x, axis, by):
    length = lax.axis_size(axis)
    pairs = [(i, i + by) for i in range(length) if 0 <= i + by < length]
    return lax.ppermute(x, axis, pairs)


def swish_value(operand):
    return operand * jax.nn.sigmoid(operand)


def swish_slope(operand):
    logistic = jax.nn.sigmoid(operand)
    return logistic * (1.0 + operand * (1.0 - logistic))


def product_nt(first_op, second_op):
    return lax.dot_general(
        first_op, second_op, (((1,), (1,)), ((), ())), preferred_element_type=jnp.float32
    )


def product_tn(first_op, second_op):
    return lax.dot_general(
        first_op, second_op, (((0,), (0,)), ((), ())), preferred_element_type=jnp.float32
    )


def shards(
    hidden,
    norm_gain,
    zx_proj,
    bc_proj,
    dt_proj,
    conv_x,
    conv_bc,
    dt_bias,
    a_log,
    d_skip,
    gate_gain,
    out_proj,
    cotangent,
):
    tokens = hidden.shape[0]
    model_width = hidden.shape[1]
    inner_local = zx_proj.shape[2]
    heads_local = dt_proj.shape[1]
    head_size = inner_local // heads_local
    state_size = bc_proj.shape[1] // 2
    inner_total = inner_local * lax.axis_size("tensor")
    blocks = tokens // BLOCK_LEN
    position = lax.axis_index("dp") % SEQ_DEVS
    opens_seq = position == 0
    closes_seq = position == SEQ_DEVS - 1
    residual = hidden.astype(jnp.float32)
    inv_rms = lax.rsqrt(jnp.mean(residual * residual, axis=1, keepdims=True) + EPSILON)
    normed = residual * inv_rms
    normed_low = (normed * norm_gain).astype(jnp.bfloat16)
    zx_flat = zx_proj.reshape(model_width, 2 * inner_local)
    zx_out = jnp.dot(normed_low, zx_flat, preferred_element_type=jnp.float32)
    gate_low = zx_out[:, :inner_local].astype(jnp.bfloat16)
    bc_out = jnp.dot(normed_low, bc_proj, preferred_element_type=jnp.float32)
    dt_raw = jnp.dot(normed_low, dt_proj, preferred_element_type=jnp.float32)
    conv_in = jnp.concatenate(
        [zx_out[:, inner_local:].astype(jnp.bfloat16), bc_out.astype(jnp.bfloat16)], axis=1
    )
    conv_weights = jnp.concatenate([conv_x, conv_bc], axis=1)
    rim_rows = shifted(conv_in[tokens - (KCONV - 1) :], "dp", 1)
    rim_rows = jnp.where(opens_seq, jnp.zeros_like(rim_rows), rim_rows)
    padded = jnp.concatenate([rim_rows, conv_in], axis=0).astype(jnp.float32)
    conv_pre = conv_weights[KCONV] + conv_weights[0] * padded[0:tokens]
    for tap_index in range(1, KCONV):
        conv_pre = conv_pre + conv_weights[tap_index] * padded[tap_index : tap_index + tokens]
    conv_act = swish_value(conv_pre)
    inputs = conv_act[:, :inner_local].reshape(blocks, BLOCK_LEN, heads_local, head_size)
    b_rows = conv_act[:, inner_local : inner_local + state_size].reshape(
        blocks, BLOCK_LEN, state_size
    )
    c_rows = conv_act[:, inner_local + state_size :].reshape(blocks, BLOCK_LEN, state_size)
    dt_pre = dt_raw + dt_bias
    step_size = jax.nn.softplus(dt_pre)
    decay_rate = -jnp.exp(a_log)
    step_blocks = step_size.reshape(blocks, BLOCK_LEN, heads_local)
    cumulative = jnp.cumsum(
        (decay_rate * step_size).reshape(blocks, BLOCK_LEN, heads_local), axis=1
    )
    cumul_heads = jnp.swapaxes(cumulative, 1, 2)
    step_heads = jnp.swapaxes(step_blocks, 1, 2)
    row_index = lax.broadcasted_iota(jnp.int32, (BLOCK_LEN, BLOCK_LEN), 0)
    col_index = lax.broadcasted_iota(jnp.int32, (BLOCK_LEN, BLOCK_LEN), 1)
    within = (row_index >= col_index)[None, None, :, :]
    spread = cumul_heads[:, :, :, None] - cumul_heads[:, :, None, :]
    decay_pairs = jnp.where(within, jnp.exp(jnp.where(within, spread, 0.0)), 0.0)
    affinity = jnp.einsum("kin,kjn->kij", c_rows, b_rows, precision=PRECISE)
    pair_weight = decay_pairs * step_heads[:, :, None, :]
    mixing = affinity[:, None, :, :] * pair_weight
    intra_out = jnp.einsum("khij,kjhp->kihp", mixing, inputs, precision=PRECISE)
    end_exp = jnp.exp(cumulative[:, -1:, :] - cumulative)
    to_end = end_exp * step_blocks
    sent_state = jnp.einsum("kjhp,kjn->khpn", to_end[..., None] * inputs, b_rows, precision=PRECISE)
    block_decay = jnp.exp(cumulative[:, -1, :])
    zero_state = jnp.zeros((heads_local, head_size, state_size), jnp.float32)
    local_in = [zero_state]
    decay_before = [jnp.ones((heads_local,), jnp.float32)]
    for block_index in range(blocks):
        local_in.append(
            block_decay[block_index][:, None, None] * local_in[-1] + sent_state[block_index]
        )
        decay_before.append(decay_before[-1] * block_decay[block_index])
    own_state = local_in[blocks]
    own_decay = decay_before[blocks]
    entry_decay = jnp.where(opens_seq, 0.0, own_decay)

    def relay_state(turn_index, incoming):
        return shifted(entry_decay[:, None, None] * incoming + own_state, "dp", 1)

    arrived = lax.fori_loop(0, SEQ_DEVS - 1, relay_state, jnp.zeros_like(own_state))
    arrived = jnp.where(opens_seq, 0.0, arrived)
    states_in = (
        jnp.stack(local_in[:blocks]) + jnp.stack(decay_before[:blocks])[:, :, None, None] * arrived
    )
    exp_cumul = jnp.exp(cumulative)
    inter_out = exp_cumul[..., None] * jnp.einsum(
        "kin,khpn->kihp", c_rows, states_in, precision=PRECISE
    )
    ssd_out = intra_out + inter_out + d_skip[:, None] * inputs
    ssd_flat = ssd_out.reshape(tokens, inner_local)
    gate_wide = gate_low.astype(jnp.float32)
    gate_act = swish_value(gate_wide)
    gated_out = ssd_flat * gate_act
    gated_low = (gated_out * gate_gain).astype(jnp.bfloat16)
    partial_proj = product_nt(gated_low, out_proj)
    proj_sum, square_sum = lax.psum(
        (partial_proj, jnp.sum(gated_out * gated_out, axis=1)), "tensor"
    )
    inv_gate = lax.rsqrt(square_sum / inner_total + EPSILON)[:, None]
    block_out = (residual + inv_gate * proj_sum).astype(jnp.bfloat16)
    grad_top = cotangent.astype(jnp.float32)
    grad_proj = (inv_gate * grad_top).astype(jnp.bfloat16)
    grad_inv = jnp.sum(grad_top * proj_sum, axis=1, keepdims=True)
    grad_gated_low = jnp.dot(grad_proj, out_proj, preferred_element_type=jnp.float32)
    grad_out_local = product_tn(grad_proj, gated_low)
    grad_gate_gain = jnp.sum(grad_gated_low * gated_out, axis=0)
    grad_gated = (
        grad_gated_low * gate_gain
        - grad_inv * inv_gate * inv_gate * inv_gate / inner_total * gated_out
    )
    grad_ssd = (grad_gated * gate_act).reshape(blocks, BLOCK_LEN, heads_local, head_size)
    grad_gate = (grad_gated * ssd_flat * swish_slope(gate_wide)).astype(jnp.bfloat16)
    grad_skip = jnp.sum(grad_ssd * inputs, axis=(0, 1, 3))
    grad_scaled = grad_ssd * exp_cumul[..., None]
    grad_c = jnp.einsum("kihp,khpn->kin", grad_scaled, states_in, precision=PRECISE)
    grad_from_out = jnp.einsum("kihp,kin->khpn", grad_scaled, c_rows, precision=PRECISE)
    grad_cumul = jnp.sum(grad_ssd * inter_out, axis=3)
    grad_mixing = jnp.einsum("kihp,kjhp->khij", grad_ssd, inputs, precision=PRECISE)
    grad_inputs = d_skip[:, None] * grad_ssd + jnp.einsum(
        "khij,kihp->kjhp", mixing, grad_ssd, precision=PRECISE
    )
    grad_affinity = jnp.sum(grad_mixing * pair_weight, axis=1)
    grad_pairs = grad_mixing * affinity[:, None, :, :] * decay_pairs
    grad_step = jnp.swapaxes(jnp.sum(grad_pairs, axis=2), 1, 2)
    grad_spread = grad_pairs * step_heads[:, :, None, :]
    grad_cumul = grad_cumul + jnp.swapaxes(
        jnp.sum(grad_spread, axis=3) - jnp.sum(grad_spread, axis=2), 1, 2
    )
    grad_c = grad_c + jnp.einsum("kij,kjn->kin", grad_affinity, b_rows, precision=PRECISE)
    grad_b = jnp.einsum("kij,kin->kjn", grad_affinity, c_rows, precision=PRECISE)
    local_grad = [zero_state]
    decay_after = [jnp.ones((heads_local,), jnp.float32)]
    for block_index in reversed(range(blocks)):
        local_grad.insert(
            0, grad_from_out[block_index] + block_decay[block_index][:, None, None] * local_grad[0]
        )
        decay_after.insert(0, decay_after[0] * block_decay[block_index])
    own_grad = local_grad[0]
    exit_decay = jnp.where(closes_seq, 0.0, own_decay)

    def relay_grad(turn_index, incoming):
        return shifted(exit_decay[:, None, None] * incoming + own_grad, "dp", -1)

    back_arrived = lax.fori_loop(0, SEQ_DEVS - 1, relay_grad, jnp.zeros_like(own_grad))
    back_arrived = jnp.where(closes_seq, 0.0, back_arrived)
    grad_states = jnp.stack(local_grad) + jnp.stack(decay_after)[:, :, None, None] * back_arrived
    grad_send = grad_states[1:]
    state_back = jnp.einsum("khpn,kjn->kjhp", grad_send, b_rows, precision=PRECISE)
    grad_to_end = jnp.sum(inputs * state_back, axis=3)
    grad_inputs = grad_inputs + to_end[..., None] * state_back
    grad_b = grad_b + jnp.einsum(
        "kjhp,khpn->kjn", to_end[..., None] * inputs, grad_send, precision=PRECISE
    )
    grad_step = grad_step + grad_to_end * end_exp
    weighted = grad_to_end * to_end
    grad_last = jnp.sum(weighted, axis=1) + block_decay * jnp.sum(
        grad_send * states_in, axis=(2, 3)
    )
    grad_cumul = (grad_cumul - weighted).at[:, -1, :].add(grad_last)
    grad_log = jnp.flip(jnp.cumsum(jnp.flip(grad_cumul, 1), axis=1), 1).reshape(tokens, heads_local)
    grad_a_log = decay_rate * jnp.sum(grad_log * step_size, axis=0)
    grad_dt_pre = (grad_step.reshape(tokens, heads_local) + decay_rate * grad_log) * jax.nn.sigmoid(
        dt_pre
    )
    grad_dt_bias = jnp.sum(grad_dt_pre, axis=0)
    grad_dt_low = grad_dt_pre.astype(jnp.bfloat16)
    grad_bc_act = lax.psum(
        jnp.concatenate([grad_b, grad_c], axis=2).reshape(tokens, 2 * state_size), "tensor"
    )
    grad_act = jnp.concatenate([grad_inputs.reshape(tokens, inner_local), grad_bc_act], axis=1)
    grad_pre = grad_act * swish_slope(conv_pre)
    rim_back = shifted(grad_pre[: KCONV - 1], "dp", -1)
    rim_back = jnp.where(closes_seq, 0.0, rim_back)
    extended = jnp.concatenate([grad_pre, rim_back], axis=0)
    grad_conv_in = conv_weights[0] * extended[KCONV - 1 : KCONV - 1 + tokens]
    for tap_index in range(1, KCONV):
        grad_conv_in = (
            grad_conv_in
            + conv_weights[tap_index]
            * extended[KCONV - 1 - tap_index : KCONV - 1 - tap_index + tokens]
        )
    grad_taps = jnp.stack(
        [
            jnp.sum(grad_pre * padded[tap_index : tap_index + tokens], axis=0)
            for tap_index in range(KCONV)
        ]
        + [jnp.sum(grad_pre, axis=0)]
    )
    grad_inner_low = grad_conv_in[:, :inner_local].astype(jnp.bfloat16)
    grad_bc_low = grad_conv_in[:, inner_local:].astype(jnp.bfloat16)
    grad_zx_low = jnp.concatenate([grad_gate, grad_inner_low], axis=1)
    grad_normed_part = product_nt(grad_zx_low, zx_flat) + product_nt(grad_dt_low, dt_proj)
    grad_normed = lax.psum(grad_normed_part, "tensor") + product_nt(grad_bc_low, bc_proj)
    grad_norm_local = jnp.sum(grad_normed * normed, axis=0)
    grad_scaled_in = grad_normed * norm_gain
    grad_resid = inv_rms * (
        grad_scaled_in - normed * jnp.mean(grad_scaled_in * normed, axis=1, keepdims=True)
    )
    grad_hidden = (grad_top + grad_resid).astype(jnp.bfloat16)
    grad_zx_local = product_tn(normed_low, grad_zx_low).reshape(model_width, 2, inner_local)
    grad_bc_local = product_tn(normed_low, grad_bc_low)
    grad_dt_local = product_tn(normed_low, grad_dt_low)
    grad_zx_proj, grad_bc_proj, grad_dt_proj, grad_out_proj = (
        lax.psum_scatter(grad_zx_local, "dp", scatter_dimension=0, tiled=True),
        lax.psum_scatter(grad_bc_local, "dp", scatter_dimension=0, tiled=True),
        lax.psum_scatter(grad_dt_local, "dp", scatter_dimension=0, tiled=True),
        lax.psum_scatter(grad_out_local, "dp", scatter_dimension=0, tiled=True),
    )
    (
        grad_norm_gain,
        grad_conv_x,
        grad_conv_bc,
        grad_dt_bias,
        grad_a_log,
        grad_d_skip,
        grad_gate_gain,
    ) = lax.psum(
        (
            grad_norm_local,
            grad_taps[:, :inner_local],
            grad_taps[:, inner_local:],
            grad_dt_bias,
            grad_a_log,
            grad_skip,
            grad_gate_gain,
        ),
        "dp",
    )
    return (
        block_out,
        grad_hidden,
        grad_norm_gain,
        grad_zx_proj,
        grad_bc_proj,
        grad_dt_proj,
        grad_conv_x,
        grad_conv_bc,
        grad_dt_bias,
        grad_a_log,
        grad_d_skip,
        grad_gate_gain,
        grad_out_proj,
    )


def solution(mesh):
    in_specs = (
        P("dp", None),
        P(),
        P(None, None, "tensor"),
        P(),
        P(None, "tensor"),
        P(None, "tensor"),
        P(),
        P("tensor"),
        P("tensor"),
        P("tensor"),
        P("tensor"),
        P(None, "tensor"),
        P("dp", None),
    )
    out_specs = (
        P("dp", None),
        P("dp", None),
        P(),
        P("dp", None, "tensor"),
        P("dp", None),
        P("dp", "tensor"),
        P(None, "tensor"),
        P(),
        P("tensor"),
        P("tensor"),
        P("tensor"),
        P("tensor"),
        P("dp", "tensor"),
    )
    return jax.shard_map(shards, mesh=mesh, in_specs=in_specs, out_specs=out_specs, check_vma=False)
```

profile of v0, /device:TPU:0, one launch (start us, length us, event | category | flops | bytes accessed | tf_op | source)
XLA Modules:
  0.0 1144.8 jit_solution(1173458592556442112)
XLA Ops:
  15.6 5.2 convolution_convert_fusion
  46.4 4.0 fusion.41
  58.0 5.1 reshape.184
  63.2 5.0 fusion.57
  69.6 59.2 %while.21 = (s32[]{:T(128)}, f32[12,64,128]{2,1,0:T(8,128)S(1)}, f32[12]{0:T(128)S(1)}, f32[12,64,128]{2,1,0:T(8,128)S(1)}, s32[]{:T(128)}) while((s32[]{:T(128)}, f32[12,64,128]{2,1,0:T(8,128)S(1)}, f32[12]{0:T(128)S(1)}, f32[12,64,128]{2,1,0:T(8,128)S(1)}, s32[]{:T(128)}) %tuple.107), condition=%wide.region_4.5_spmd, body=%wide.region_3.4_spmd.sunk | while | flops 196610 | bytes 2752661 | solution.py:128
  69.8 4.6 collective-permute-start
  75.8 5.3 collective-permute-start
  82.6 7.8 collective-permute-start
  91.8 7.8 collective-permute-start
  101.0 7.8 collective-permute-start
  110.2 7.8 collective-permute-start
  119.4 7.8 collective-permute-start
  134.9 15.0 %fusion.50 = f32[4,256,12,64]{1,3,2,0:T(8,128)S(1)} fusion(f32[4,256,12,64]{1,3,2,0:T(8,128)S(1)} %fusion.134, f32[4,256,12,64]{1,0,3,2:T(4,128)S(1)} %copy-done.4, f32[4,12,256]{2,1,0:T(8,128)S(1)} %copy-done.59, f32[4,12,256]{2,1,0:T(8,128)S(1)} %copy-done.58, f32[4,256,256]{2,1,0:T(8,128)S(1)} %fusion.141, pred[256,256]{1,0:T(8,128)(4,1)S(1)} %copy-done.61, ...), kind=kOutput, calls=%fused_computation.80 | convolution fusion | flops 2434793472 | bytes 10698800 | tf_op jit(solution)/shard_map/khij,kjhp->kihp/dot_general | solution.py:108
  163.2 4.6 fusion.100
  168.5 12.0 %psum.77 = f32[1024]{0:T(1024)S(1)} all-reduce(f32[1024]{0:T(1024)S(1)} %get-tuple-element.116), channel_id=1, replica_groups=mesh['dp'=8,'tensor'=4] {'tensor'}, use_global_device_ids=true, to_apply=%region_6.7 | all-reduce | flops 1024 | bytes 8192 | tf_op jit(solution)/shard_map/psum | solution.py:144
  180.6 223.6 %all-reduce.7.cloned.1.call-done = f32[1024,1536]{1,0:T(8,128)} async-done(((f32[1024,1536]{1,0:T(8,128)}), f32[1024,1536]{1,0:T(8,128)}) %all-reduce.7.cloned.1.call-update) | async-done | bytes 6291472 | tf_op jit(solution)/shard_map/psum | solution.py:144
  404.2 7.0 fusion.18
  413.9 7.6 multiply_reduce_fusion.8
  425.1 5.2 reshape.192
  430.4 5.0 fusion.53
  436.7 65.4 %while.22 = (s32[]{:T(128)}, f32[12,64,128]{2,1,0:T(8,128)S(1)}, f32[12]{0:T(128)S(1)}, f32[12,64,128]{2,1,0:T(8,128)S(1)}, s32[]{:T(128)}) while((s32[]{:T(128)}, f32[12,64,128]{2,1,0:T(8,128)S(1)}, f32[12]{0:T(128)S(1)}, f32[12,64,128]{2,1,0:T(8,128)S(1)}, s32[]{:T(128)}) %tuple.106), condition=%wide.region_10.11_spmd, body=%wide.region_9.10_spmd.sunk | while | flops 196610 | bytes 2752661 | solution.py:192
  443.6 7.3 collective-permute-done.1
  453.1 8.0 collective-permute-done.1
  463.2 8.0 collective-permute-done.1
  473.4 8.0 collective-permute-done.1
  483.5 8.0 collective-permute-done.1
  493.7 8.0 collective-permute-done.1
  507.6 4.8 multiply_reduce_fusion.10
  515.9 20.0 %multiply_reduce_fusion.1 = (f32[4,12,256]{2,1,0:T(8,128)}, f32[4,12,256]{2,1,0:T(8,128)}, f32[4,12,256]{2,1,0:T(8,128)}, f32[4,256,256]{2,1,0:T(8,128)S(1)}) fusion(f32[4,12,256]{2,1,0:T(8,128)S(1)} %copy-done.59, f32[4,12,256]{2,1,0:T(8,128)S(1)} %copy-done.58, pred[256,256]{1,0:T(8,128)(4,1)S(1)} %copy-done.62, f32[4,256,256]{2,1,0:T(8,128)S(1)} %copy-done.48, ...), kind=kOutput, calls=%fused_computation.9 | convolution fusion | flops 2453368832 | bytes 8699904 | tf_op jit(solution)/shard_map/kihp,kjhp->khij/dot_general | solution.py:166
  540.5 12.9 %fusion.49 = f32[4,256,12,64]{1,3,2,0:T(8,128)} fusion(f32[4,256,12,64]{1,3,2,0:T(8,128)S(1)} %get-tuple-element.158, f32[4,256,12,64]{1,0,3,2:T(4,128)S(1)} %copy-done.9, f32[4,12,256]{2,1,0:T(8,128)S(1)} %copy-done.60, f32[4,12,256]{2,1,0:T(8,128)S(1)} %copy-done.58, f32[4,256,256]{2,1,0:T(8,128)S(1)} %copy-done.48, pred[256,256]{1,0:T(8,128)(4,1)S(1)} %copy-done.62, ...), kind=kOutput, calls=%fused_computation.78 | convolution fusion | flops 2434793472 | bytes 10698800 | tf_op jit(solution)/shard_map/khij,kihp->kjhp/dot_general | solution.py:167
  567.5 4.2 multiply_reduce_fusion.13
  578.1 3.7 copy.290
  586.2 35.3 %all-reduce.9.cloned.1.call-done = f32[1024,256]{1,0:T(8,128)} async-done(((f32[1024,256]{1,0:T(8,128)}), f32[1024,256]{1,0:T(8,128)}) %all-reduce.9.cloned.1.call-update) | async-done | bytes 1048592 | tf_op jit(solution)/shard_map/psum | solution.py:215
  621.6 10.5 multiply_reduce_fusion.3
  637.6 7.6 fusion.37
  647.7 7.5 fusion.69
  655.3 15.0 %copy.307 = f32[1536,2,768]{2,1,0:T(2,128)} copy(f32[1536,2,768]{0,2,1:T(8,128)} %bitcast.208) | data formatting | bytes 18874368 | tf_op jit(solution)/shard_map/reshape | solution.py:248
  670.3 7.9 fusion.70
  678.3 4.0 convolution_add_fusion.1
  682.9 7.9 fusion.83
  693.0 4.1 fusion.102
  698.9 114.5 %all-reduce.13.cloned.1.call-done = f32[1536,2,768]{2,1,0:T(2,128)} async-done(((f32[1536,2,768]{2,1,0:T(2,128)}), f32[1536,2,768]{2,1,0:T(2,128)}) %all-reduce.13.cloned.1.call-update) | async-done | bytes 9437200
  816.1 222.5 %all-reduce.11.cloned.1.call-done = f32[1024,1536]{1,0:T(8,128)} async-done(((f32[1024,1536]{1,0:T(8,128)}), f32[1024,1536]{1,0:T(8,128)}) %all-reduce.11.cloned.1.call-update) | async-done | bytes 6291472 | tf_op jit(solution)/shard_map/psum | solution.py:241
  1038.6 6.5 fusion.14
  1045.1 25.4 %all-reduce.1 = (f32[1536]{0:T(1024)}, f32[5,768]{1,0:T(8,128)}, f32[5,256]{1,0:T(8,128)}, f32[12]{0:T(128)}, f32[12]{0:T(128)}, /*index=5*/f32[12]{0:T(128)}, f32[768]{0:T(1024)}) all-reduce(f32[1536]{0:T(1024)S(1)} %get-tuple-element.75, f32[5,768]{1,0:T(8,128)S(1)} %slice.249, ...), channel_id=1, replica_groups=mesh['dp'=8,'tensor'=4] {'dp'}, use_global_device_ids=true, to_apply=%region_25.26 | all-reduce | flops 7460 | bytes 59680 | tf_op jit(solution)/shard_map/psum | solution.py:265
  1070.5 7.0 fusion.19
  1077.5 17.7 %reduce-scatter.8.cloned.1.call-done = f32[192,768]{1,0:T(8,128)} async-done(((f32[1536,768]{1,0:T(8,128)}), f32[192,768]{1,0:T(8,128)}) %reduce-scatter.8.cloned.1.call-update) | async-done | bytes 589840 | tf_op jit(solution)/shard_map/reduce_scatter | solution.py:255
  1095.2 42.2 %reduce-scatter.6.cloned.1.call-done = f32[192,256]{1,0:T(8,128)} async-done(((f32[1536,256]{1,0:T(8,128)}), f32[192,256]{1,0:T(8,128)}) %reduce-scatter.6.cloned.1.call-update) | async-done | bytes 196624 | tf_op jit(solution)/shard_map/reduce_scatter | solution.py:253
  (374 shorter events, 150.2 us)
Async XLA Ops:
  7.2 156.0 %copy-start = (bf16[1536,768]{1,0:T(8,128)(2,1)S(1)}, bf16[1536,768]{1,0:T(8,128)(2,1)}, u32[]{:S(2)}) copy-start(bf16[1536,768]{1,0:T(8,128)(2,1)} %param.30) | copy-start | bytes 7077892
  7.2 397.0 %all-reduce.7.cloned.1.call-start = ((), (), s32[]{:S(2)}) async-start(), calls=%async_computation.3 | async-start | bytes 12582912 | tf_op jit(solution)/shard_map/psum | solution.py:144
  24.5 19.6 %collective-permute-start.2 = (bf16[3,1024]{1,0:T(4,128)(2,1)S(1)}, bf16[3,1024]{1,0:T(4,128)(2,1)}, u32[]{:S(2)}, u32[]{:S(2)}) collective-permute-start(bf16[3,1024]{1,0:T(4,128)(2,1)S(1)} %pad_maximum_fusion.5), channel_id=1, source_target_pairs={{0,4},{4,8},{8,12},{12,16},{16,20},{20,24},{24,28},{1,5},{5,9},{9,... | collective-permute-start | bytes 18440 | tf_op jit(solution)/shard_map/ppermute | solution.py:16
  34.3 12.0 %copy-start.35 = (f32[4,12,256]{1,0,2:T(4,128)}, f32[4,12,256]{1,0,2:T(4,128)S(1)}, u32[]{:S(2)}) copy-start(f32[4,12,256]{1,0,2:T(4,128)S(1)} %copy.271) | copy-start | bytes 147460
  35.7 10.6 copy-start.65
  35.7 10.6 copy-start.67
  37.4 32.0 %copy-start.72 = (f32[12]{0:T(128)}, f32[12]{0:T(128)S(1)}, u32[]{:S(2)}) copy-start(f32[12]{0:T(128)S(1)} %get-tuple-element.152) | copy-start | bytes 148
  41.5 21.6 %copy-start.51 = (f32[4,256,12]{1,2,0:T(8,128)}, f32[4,256,12]{1,2,0:T(8,128)S(1)}, u32[]{:S(2)}) copy-start(f32[4,256,12]{1,2,0:T(8,128)S(1)} %copy.274) | copy-start | bytes 147460
  52.5 10.6 copy-start.15
  69.8 6.0 collective-permute-start
  75.8 6.6 collective-permute-start
  82.6 9.1 collective-permute-start
  91.8 9.1 collective-permute-start
  101.0 9.1 collective-permute-start
  110.2 9.1 collective-permute-start
  119.4 9.1 collective-permute-start
  131.2 18.7 %copy-start.47 = (f32[4,256,256]{2,1,0:T(8,128)}, f32[4,256,256]{2,1,0:T(8,128)S(1)}, u32[]{:S(2)}) copy-start(f32[4,256,256]{2,1,0:T(8,128)S(1)} %fusion.141) | copy-start | bytes 3145732
  134.9 15.1 %copy-start.21 = (f32[4,256,12,64]{1,3,2,0:T(8,128)}, f32[4,256,12,64]{1,3,2,0:T(8,128)S(1)}, u32[]{:S(2)}) copy-start(f32[4,256,12,64]{1,3,2,0:T(8,128)S(1)} %fusion.134) | copy-start | bytes 9437188
  167.8 453.7 %all-reduce.9.cloned.1.call-start = ((), (), s32[]{:S(2)}) async-start(), calls=%async_computation.4 | async-start | bytes 2097152 | tf_op jit(solution)/shard_map/psum | solution.py:215
  180.6 230.7 %copy-start.75 = (f32[1024]{0:T(1024)}, f32[1024]{0:T(1024)S(1)}, u32[]{:S(2)}) copy-start(f32[1024]{0:T(1024)S(1)} %add_rsqrt_fusion) | copy-start | bytes 12292
  404.2 8.9 copy-start.20
  404.2 9.7 copy-start.39
  437.6 3.8 collective-permute-start.1
  442.3 8.6 collective-permute-start.1
  451.8 9.3 collective-permute-start.1
  461.9 9.3 collective-permute-start.1
  472.1 9.3 collective-permute-start.1
  482.2 9.3 collective-permute-start.1
  492.4 9.3 collective-permute-start.1
  515.9 20.1 %copy-start.24 = (f32[1,12,64,128]{3,2,1,0:T(8,128)S(1)}, f32[1,12,64,128]{3,2,1,0:T(8,128)}, u32[]{:S(2)}) copy-start(f32[1,12,64,128]{3,2,1,0:T(8,128)} %get-tuple-element.120) | copy-start | bytes 1179652
  515.9 20.1 %copy-start.27 = (f32[1,12,64,128]{3,2,1,0:T(8,128)S(1)}, f32[1,12,64,128]{3,2,1,0:T(8,128)}, u32[]{:S(2)}) copy-start(f32[1,12,64,128]{3,2,1,0:T(8,128)} %get-tuple-element.121) | copy-start | bytes 1179652
  515.9 20.1 %copy-start.30 = (f32[1,12,64,128]{3,2,1,0:T(8,128)S(1)}, f32[1,12,64,128]{3,2,1,0:T(8,128)}, u32[]{:S(2)}) copy-start(f32[1,12,64,128]{3,2,1,0:T(8,128)} %get-tuple-element.122) | copy-start | bytes 1179652
  515.9 20.1 %copy-start.33 = (f32[1,12,64,128]{3,2,1,0:T(8,128)S(1)}, f32[1,12,64,128]{3,2,1,0:T(8,128)}, u32[]{:S(2)}) copy-start(f32[1,12,64,128]{3,2,1,0:T(8,128)} %copy-done.32) | copy-start | bytes 1179652
  559.6 137.6 %reduce-scatter.10.cloned.1.call-start = ((), (), s32[]{:S(2)}) async-start(), calls=%async_computation.8 | async-start | bytes 884736
  561.9 9.9 copy-start.25
  561.9 9.9 copy-start.28
  621.6 13.7 %copy-start.7 = (bf16[1024,1536]{1,0:T(8,128)(2,1)S(1)}, bf16[1024,1536]{1,0:T(8,128)(2,1)}, u32[]{:S(2)}) copy-start(bf16[1024,1536]{1,0:T(8,128)(2,1)} %copy-done.6) | copy-start | bytes 9437188
  634.0 3.6 collective-permute-start.3
  637.3 176.1 %all-reduce.13.cloned.1.call-start = ((), (), s32[]{:S(2)}) async-start(), calls=%async_computation.9 | async-start | bytes 18874368
  645.4 9.9 copy-start.45
  670.3 368.3 %all-reduce.11.cloned.1.call-start = ((), (), s32[]{:S(2)}) async-start(), calls=%async_computation.5 | async-start | bytes 12582912 | tf_op jit(solution)/shard_map/psum | solution.py:241
  682.3 412.9 %reduce-scatter.8.cloned.1.call-start = ((), (), s32[]{:S(2)}) async-start(), calls=%async_computation.7 | async-start | bytes 5308416 | tf_op jit(solution)/shard_map/reduce_scatter | solution.py:255
  690.9 446.5 %reduce-scatter.6.cloned.1.call-start = ((), (), s32[]{:S(2)}) async-start(), calls=%async_computation.6 | async-start | bytes 1769472 | tf_op jit(solution)/shard_map/reduce_scatter | solution.py:253
  697.1 341.5 %copy-start.50 = (bf16[1536,256]{1,0:T(8,128)(2,1)S(1)}, bf16[1536,256]{1,0:T(8,128)(2,1)}, u32[]{:S(2)}) copy-start(bf16[1536,256]{1,0:T(8,128)(2,1)} %param.22) | copy-start | bytes 2359300
  697.1 341.5 %copy-start.57 = (f32[1536]{0:T(1024)S(1)}, f32[1536]{0:T(1024)}, u32[]{:S(2)}) copy-start(f32[1536]{0:T(1024)} %param.20) | copy-start | bytes 18436
  697.1 341.5 %copy-start.64 = (f32[1024]{0:T(1024)S(1)}, f32[1024]{0:T(1024)}, u32[]{:S(2)}) copy-start(f32[1024]{0:T(1024)} %copy-done.63) | copy-start | bytes 12292
  816.1 229.0 %copy-start.88 = (f32[768]{0:T(1024)S(1)}, f32[768]{0:T(1024)}, u32[]{:S(2)}) copy-start(f32[768]{0:T(1024)} %get-tuple-element.126) | copy-start | bytes 9220
  1070.5 66.9 %copy-start.1 = (bf16[1536,768]{1,0:T(8,128)(2,1)S(1)}, bf16[1536,768]{1,0:T(8,128)(2,1)}, u32[]{:S(2)}) copy-start(bf16[1536,768]{1,0:T(8,128)(2,1)} %param.30) | copy-start | bytes 7077892
  (80 other events, 295.5 us)
Sparse Core Ops, SparseCore 0:
  168.0 236.1 all-reduce.6
  559.7 61.8 all-reduce.8
  637.4 34.9 reduce-scatter.9
  675.7 137.6 all-reduce.12
  815.6 222.9 all-reduce.10
  1042.4 52.7 reduce-scatter.7
  1099.1 38.3 reduce-scatter.5
where the time goes:
time: 1150 us; the launch traced here: 1140 us
  waiting for transfers between devices  715 us (62%)
  matrix products  139 us (12%)
  local copies, waits for them, and re-layouts  97 us (8%)
  other arithmetic  75.5 us (7%)
  starting transfers between devices  63.3 us (6%)
  blocking collectives  37.4 us (3%)
  between operations  16.7 us (1%)
    psum x1, waiting for transfers between devices, shards(): lax.psum((partial_proj, jnp.sum(gated_out * gated_out, axis=1)), 'tensor')  224 us
    psum x1, waiting for transfers between devices, shards(): lax.psum(grad_normed_part, 'tensor') + product_nt(grad_bc_low, bc_proj)  222 us
    unnamed x9, waiting for transfers between devices  115 us
    ppermute x16, starting transfers between devices, shifted(): return lax.ppermute(x, axis, pairs)  62.3 us
    ppermute x16, waiting for transfers between devices, shifted(): return lax.ppermute(x, axis, pairs)  59 us
    reduce_scatter x1, waiting for transfers between devices, shards(): lax.psum_scatter(grad_bc_local, 'dp', scatter_dimension=0, tiled=True)  42.2 us
    psum x1, waiting for transfers between devices, shards(): lax.psum(jnp.concatenate([grad_b, grad_c], axis=2).reshape(tokens, 2 * st...  35.3 us
    unnamed x222, local copies, waits for them, and re-layouts  32 us
  transfers between devices with their start and end apart: 23, of which 20 were waited for; matrix products, arithmetic and copies ran while one was open for 10% of the time, Pallas kernels for 0%

commit v1 on v0

--- a/solution.py
+++ b/solution.py
@@ -212,9 +212,8 @@
     )
     grad_dt_bias = jnp.sum(grad_dt_pre, axis=0)
     grad_dt_low = grad_dt_pre.astype(jnp.bfloat16)
-    grad_bc_act = lax.psum(
-        jnp.concatenate([grad_b, grad_c], axis=2).reshape(tokens, 2 * state_size), "tensor"
-    )
+    state = jnp.concatenate([grad_b, grad_c], axis=2).reshape(tokens, 2 * state_size)
+    grad_bc_act = lax.all_gather(state, axis_name="tensor").sum(axis=0)
     grad_act = jnp.concatenate([grad_inputs.reshape(tokens, inner_local), grad_bc_act], axis=1)
     grad_pre = grad_act * swish_slope(conv_pre)
     rim_back = shifted(grad_pre[: KCONV - 1], "dp", -1)

time: 1150 us -> 1160 us (level)
    all_gather x0 -> x1, waiting for transfers between devices: none -> 43.1 us  [shards(): grad_bc_act = lax.all_gather(state, axis_name='tensor').sum(axis=0)]
    psum x1 -> x0, waiting for transfers between devices: 35.3 us -> none  [shards(): lax.psum(jnp.concatenate([grad_b, grad_c], axis=2).reshape(tokens, 2 * st...]
    unnamed x222 -> x244, local copies, waits for them, and re-layouts: 32 us -> 31.2 us
  transfers between devices with their start and end apart: 23 -> 23, of which waited for: 20 -> 20; matrix products, arithmetic and copies ran while one was open for 10% -> 12% of each run, Pallas kernels for 0% -> 0%
where the time goes in v1:
time: 1160 us
  waiting for transfers between devices  721 us (62%)
  matrix products  142 us (12%)
  local copies, waits for them, and re-layouts  97.5 us (8%)
  other arithmetic  77.7 us (7%)
  starting transfers between devices  63.5 us (5%)
  blocking collectives  37.3 us (3%)
  between operations  16.6 us (1%)
    psum x1, waiting for transfers between devices, shards(): lax.psum((partial_proj, jnp.sum(gated_out * gated_out, axis=1)), 'tensor')  224 us
    psum x1, waiting for transfers between devices, shards(): lax.psum(grad_normed_part, 'tensor') + product_nt(grad_bc_low, bc_proj)  222 us
    unnamed x9, waiting for transfers between devices  114 us
    ppermute x16, starting transfers between devices, shifted(): return lax.ppermute(x, axis, pairs)  62.8 us
    ppermute x16, waiting for transfers between devices, shifted(): return lax.ppermute(x, axis, pairs)  57.6 us
    all_gather x1, waiting for transfers between devices, shards(): grad_bc_act = lax.all_gather(state, axis_name='tensor').sum(axis=0)  43.1 us
    reduce_scatter x1, waiting for transfers between devices, shards(): lax.psum_scatter(grad_bc_local, 'dp', scatter_dimension=0, tiled=True)  42.2 us
    unnamed x244, local copies, waits for them, and re-layouts  31.2 us
  transfers between devices with their start and end apart: 23, of which 20 were waited for; matrix products, arithmetic and copies ran while one was open for 12% of the time, Pallas kernels for 0%

profile of v1, /device:TPU:0, one launch (start us, length us, event | category | flops | bytes accessed | tf_op | source)
XLA Modules:
  0.0 1156.7 jit_solution(5371803938681601307)
XLA Ops:
  15.6 5.2 convolution_convert_fusion
  46.5 4.0 fusion.41
  58.1 5.1 reshape.181
  63.3 5.0 fusion.57
  69.8 59.3 %while.21 = (s32[]{:T(128)}, f32[12,64,128]{2,1,0:T(8,128)S(1)}, f32[12]{0:T(128)S(1)}, f32[12,64,128]{2,1,0:T(8,128)S(1)}, s32[]{:T(128)}) while((s32[]{:T(128)}, f32[12,64,128]{2,1,0:T(8,128)S(1)}, f32[12]{0:T(128)S(1)}, f32[12,64,128]{2,1,0:T(8,128)S(1)}, s32[]{:T(128)}) %tuple.106), condition=%wide.region_4.5_spmd, body=%wide.region_3.4_spmd.sunk | while | flops 196610 | bytes 2752661 | solution.py:128
  69.9 4.6 collective-permute-start
  76.0 5.3 collective-permute-start
  82.7 7.8 collective-permute-start
  91.9 7.8 collective-permute-start
  101.1 7.8 collective-permute-start
  110.3 7.8 collective-permute-start
  119.5 7.8 collective-permute-start
  134.5 15.0 %fusion.50 = f32[4,256,12,64]{1,3,2,0:T(8,128)S(1)} fusion(f32[4,256,12,64]{1,3,2,0:T(8,128)S(1)} %fusion.134, f32[4,256,12,64]{1,0,3,2:T(4,128)S(1)} %copy-done.4, f32[4,12,256]{2,1,0:T(8,128)S(1)} %copy-done.71, f32[4,12,256]{2,1,0:T(8,128)S(1)} %copy-done.68, f32[4,256,256]{2,1,0:T(8,128)S(1)} %fusion.141, pred[256,256]{1,0:T(8,128)(4,1)S(1)} %copy-done.74, ...), kind=kOutput, calls=%fused_computation.80 | convolution fusion | flops 2434793472 | bytes 10698800 | tf_op jit(solution)/shard_map/khij,kjhp->kihp/dot_general | solution.py:108
  162.7 4.6 fusion.100
  168.0 12.0 %psum.70 = f32[1024]{0:T(1024)S(1)} all-reduce(f32[1024]{0:T(1024)S(1)} %get-tuple-element.116), channel_id=1, replica_groups=mesh['dp'=8,'tensor'=4] {'tensor'}, use_global_device_ids=true, to_apply=%region_6.7 | all-reduce | flops 1024 | bytes 8192 | tf_op jit(solution)/shard_map/psum | solution.py:144
  180.0 223.6 %all-reduce.6.cloned.1.call-done = f32[1024,1536]{1,0:T(8,128)} async-done(((f32[1024,1536]{1,0:T(8,128)}), f32[1024,1536]{1,0:T(8,128)}) %all-reduce.6.cloned.1.call-update) | async-done | bytes 6291472 | tf_op jit(solution)/shard_map/psum | solution.py:144
  403.6 7.0 fusion.18
  413.4 7.6 multiply_reduce_fusion.8
  424.6 5.2 reshape.189
  429.8 5.1 fusion.53
  437.5 20.6 %multiply_reduce_fusion.1 = (f32[4,12,256]{2,1,0:T(8,128)}, f32[4,12,256]{2,1,0:T(8,128)}, f32[4,12,256]{2,1,0:T(8,128)}, f32[4,256,256]{2,1,0:T(8,128)}) fusion(f32[4,12,256]{2,1,0:T(8,128)S(1)} %copy-done.72, f32[4,12,256]{2,1,0:T(8,128)S(1)} %copy-done.69, pred[256,256]{1,0:T(8,128)(4,1)S(1)} %copy-done.75, f32[4,256,256]{2,1,0:T(8,128)S(1)} %copy-done.56, ...), kind=kOutput, calls=%fused_computation.9 | convolution fusion | flops 2453368832 | bytes 8699904 | tf_op jit(solution)/shard_map/kihp,kjhp->khij/dot_general | solution.py:166
  458.1 4.2 fusion.90
  462.4 62.5 %while.22 = (s32[]{:T(128)}, f32[12,64,128]{2,1,0:T(8,128)S(1)}, f32[12]{0:T(128)}, f32[12,64,128]{2,1,0:T(8,128)S(1)}, s32[]{:T(128)}) while((s32[]{:T(128)}, f32[12,64,128]{2,1,0:T(8,128)S(1)}, f32[12]{0:T(128)}, f32[12,64,128]{2,1,0:T(8,128)S(1)}, s32[]{:T(128)}) %tuple.89), condition=%wide.region_10.11_spmd, body=%wide.region_9.10_spmd.sunk | while | flops 196610 | bytes 2752661 | solution.py:192
  468.7 7.2 collective-permute-done.1
  477.9 7.8 collective-permute-done.1
  487.7 7.8 collective-permute-done.1
  497.5 7.8 collective-permute-done.1
  507.3 7.8 collective-permute-done.1
  517.1 7.8 collective-permute-done.1
  529.7 4.9 fusion.87
  541.0 5.9 multiply_reduce_fusion.10
  547.0 12.2 %fusion.49 = f32[4,256,12,64]{1,3,2,0:T(8,128)S(1)} fusion(f32[4,256,12,64]{1,3,2,0:T(8,128)S(1)} %get-tuple-element.158, f32[4,256,12,64]{1,0,3,2:T(4,128)S(1)} %copy-done.11, f32[4,12,256]{2,1,0:T(8,128)S(1)} %copy-done.73, f32[4,12,256]{2,1,0:T(8,128)S(1)} %copy-done.70, f32[4,256,256]{2,1,0:T(8,128)S(1)} %copy-done.57, ...), kind=kOutput, calls=%fused_computation.78 | convolution fusion | flops 2434793472 | bytes 10698800 | tf_op jit(solution)/shard_map/khij,kihp->kjhp/dot_general | solution.py:167
  567.2 4.6 multiply_reduce_fusion.9
  588.4 43.1 %all-gather.2.cloned.1.call-done = f32[4,1024,256]{2,1,0:T(8,128)} async-done(((f32[1,1024,256]{2,1,0:T(8,128)}), f32[4,1024,256]{2,1,0:T(8,128)}) %all-gather.2.cloned.1.call-update) | async-done | bytes 4194320 | tf_op jit(solution)/shard_map/all_gather | solution.py:216
  634.2 10.5 multiply_reduce_fusion.3
  650.4 7.4 fusion.37
  660.4 7.5 fusion.69
  667.9 14.8 %copy.306 = f32[1536,2,768]{2,1,0:T(2,128)} copy(f32[1536,2,768]{0,2,1:T(8,128)} %bitcast.208) | data formatting | bytes 18874368 | tf_op jit(solution)/shard_map/reshape | solution.py:247
  682.8 7.9 fusion.70
  695.4 7.9 fusion.83
  705.4 4.1 fusion.102
  711.4 114.3 %all-reduce.10.cloned.1.call-done = f32[1536,2,768]{2,1,0:T(2,128)} async-done(((f32[1536,2,768]{2,1,0:T(2,128)}), f32[1536,2,768]{2,1,0:T(2,128)}) %all-reduce.10.cloned.1.call-update) | async-done | bytes 9437200
  828.3 222.5 %all-reduce.8.cloned.1.call-done = f32[1024,1536]{1,0:T(8,128)} async-done(((f32[1024,1536]{1,0:T(8,128)}), f32[1024,1536]{1,0:T(8,128)}) %all-reduce.8.cloned.1.call-update) | async-done | bytes 6291472 | tf_op jit(solution)/shard_map/psum | solution.py:240
  1050.8 6.5 fusion.14
  1057.3 25.3 %all-reduce.1 = (f32[1536]{0:T(1024)}, f32[5,768]{1,0:T(8,128)}, f32[5,256]{1,0:T(8,128)}, f32[12]{0:T(128)}, f32[12]{0:T(128)}, /*index=5*/f32[12]{0:T(128)}, f32[768]{0:T(1024)}) all-reduce(f32[1536]{0:T(1024)S(1)} %get-tuple-element.75, f32[5,768]{1,0:T(8,128)S(1)} %slice.249, ...), channel_id=1, replica_groups=mesh['dp'=8,'tensor'=4] {'dp'}, use_global_device_ids=true, to_apply=%region_25.26 | all-reduce | flops 7460 | bytes 59680 | tf_op jit(solution)/shard_map/psum | solution.py:264
  1082.7 7.0 fusion.19
  1089.7 17.8 %reduce-scatter.8.cloned.1.call-done = f32[192,768]{1,0:T(8,128)} async-done(((f32[1536,768]{1,0:T(8,128)}), f32[192,768]{1,0:T(8,128)}) %reduce-scatter.8.cloned.1.call-update) | async-done | bytes 589840 | tf_op jit(solution)/shard_map/reduce_scatter | solution.py:254
  1107.5 42.2 %reduce-scatter.6.cloned.1.call-done = f32[192,256]{1,0:T(8,128)} async-done(((f32[1536,256]{1,0:T(8,128)}), f32[192,256]{1,0:T(8,128)}) %reduce-scatter.6.cloned.1.call-update) | async-done | bytes 196624 | tf_op jit(solution)/shard_map/reduce_scatter | solution.py:252
  (397 shorter events, 153.5 us)
Async XLA Ops:
  7.2 155.5 %copy-start = (bf16[1536,768]{1,0:T(8,128)(2,1)S(1)}, bf16[1536,768]{1,0:T(8,128)(2,1)}, u32[]{:S(2)}) copy-start(bf16[1536,768]{1,0:T(8,128)(2,1)} %param.30) | copy-start | bytes 7077892
  7.2 396.4 %all-reduce.6.cloned.1.call-start = ((), (), s32[]{:S(2)}) async-start(), calls=%async_computation.3 | async-start | bytes 12582912 | tf_op jit(solution)/shard_map/psum | solution.py:144
  24.5 19.6 %collective-permute-start.2 = (bf16[3,1024]{1,0:T(4,128)(2,1)S(1)}, bf16[3,1024]{1,0:T(4,128)(2,1)}, u32[]{:S(2)}, u32[]{:S(2)}) collective-permute-start(bf16[3,1024]{1,0:T(4,128)(2,1)S(1)} %pad_maximum_fusion.5), channel_id=1, source_target_pairs={{0,4},{4,8},{8,12},{12,16},{16,20},{20,24},{24,28},{1,5},{5,9},{9,... | collective-permute-start | bytes 18440 | tf_op jit(solution)/shard_map/ppermute | solution.py:16
  34.4 12.0 %copy-start.34 = (f32[4,12,256]{1,0,2:T(4,128)}, f32[4,12,256]{1,0,2:T(4,128)S(1)}, u32[]{:S(2)}) copy-start(f32[4,12,256]{1,0,2:T(4,128)S(1)} %copy.270) | copy-start | bytes 147460
  35.9 10.6 copy-start.79
  35.9 10.6 copy-start.81
  37.5 32.0 %copy-start.85 = (f32[12]{0:T(128)}, f32[12]{0:T(128)S(1)}, u32[]{:S(2)}) copy-start(f32[12]{0:T(128)S(1)} %get-tuple-element.152) | copy-start | bytes 148
  41.7 21.6 %copy-start.60 = (f32[4,256,12]{1,2,0:T(8,128)}, f32[4,256,12]{1,2,0:T(8,128)S(1)}, u32[]{:S(2)}) copy-start(f32[4,256,12]{1,2,0:T(8,128)S(1)} %copy.273) | copy-start | bytes 147460
  52.6 10.6 copy-start.17
  69.9 6.0 collective-permute-start
  76.0 6.6 collective-permute-start
  82.7 9.1 collective-permute-start
  91.9 9.1 collective-permute-start
  101.1 9.1 collective-permute-start
  110.3 9.1 collective-permute-start
  119.5 9.1 collective-permute-start
  131.5 18.0 %copy-start.55 = (f32[4,256,256]{2,1,0:T(8,128)}, f32[4,256,256]{2,1,0:T(8,128)S(1)}, u32[]{:S(2)}) copy-start(f32[4,256,256]{2,1,0:T(8,128)S(1)} %fusion.141) | copy-start | bytes 3145732
  131.7 17.9 %copy-start.32 = (f32[1,12,64,128]{3,2,1,0:T(8,128)}, f32[1,12,64,128]{3,2,1,0:T(8,128)S(1)}, u32[]{:S(2)}) copy-start(f32[1,12,64,128]{3,2,1,0:T(8,128)S(1)} %broadcast.109) | copy-start | bytes 1179652
  134.5 15.1 %copy-start.24 = (f32[4,256,12,64]{1,3,2,0:T(8,128)}, f32[4,256,12,64]{1,3,2,0:T(8,128)S(1)}, u32[]{:S(2)}) copy-start(f32[4,256,12,64]{1,3,2,0:T(8,128)S(1)} %fusion.134) | copy-start | bytes 9437188
  167.3 464.3 %all-gather.2.cloned.1.call-start = ((), (), s32[]{:S(2)}) async-start(), calls=%async_computation.4 | async-start | bytes 5242880 | tf_op jit(solution)/shard_map/all_gather | solution.py:216
  180.0 230.7 %copy-start.88 = (f32[1024]{0:T(1024)}, f32[1024]{0:T(1024)S(1)}, u32[]{:S(2)}) copy-start(f32[1024]{0:T(1024)S(1)} %add_rsqrt_fusion) | copy-start | bytes 12292
  437.4 20.6 %copy-start.28 = (f32[1,12,64,128]{3,2,1,0:T(8,128)S(1)}, f32[1,12,64,128]{3,2,1,0:T(8,128)}, u32[]{:S(2)}) copy-start(f32[1,12,64,128]{3,2,1,0:T(8,128)} %get-tuple-element.121) | copy-start | bytes 1179652
  437.4 20.6 %copy-start.31 = (f32[1,12,64,128]{3,2,1,0:T(8,128)S(1)}, f32[1,12,64,128]{3,2,1,0:T(8,128)}, u32[]{:S(2)}) copy-start(f32[1,12,64,128]{3,2,1,0:T(8,128)} %get-tuple-element.122) | copy-start | bytes 1179652
  437.4 20.6 %copy-start.33 = (f32[1,12,64,128]{3,2,1,0:T(8,128)S(1)}, f32[1,12,64,128]{3,2,1,0:T(8,128)}, u32[]{:S(2)}) copy-start(f32[1,12,64,128]{3,2,1,0:T(8,128)} %copy-done.32) | copy-start | bytes 1179652
  437.5 20.6 %copy-start.54 = (f32[4,256,12]{1,2,0:T(8,128)S(1)}, f32[4,256,12]{1,2,0:T(8,128)}, u32[]{:S(2)}) copy-start(f32[4,256,12]{1,2,0:T(8,128)} %copy.271) | copy-start | bytes 147460
  462.3 62.6 %copy-start.40 = (f32[1,12,64,128]{3,2,1,0:T(8,128)S(1)}, f32[1,12,64,128]{3,2,1,0:T(8,128)}, u32[]{:S(2)}) copy-start(f32[1,12,64,128]{3,2,1,0:T(8,128)} %get-tuple-element.115) | copy-start | bytes 1179652
  463.1 3.6 collective-permute-start.1
  467.4 8.5 collective-permute-start.1
  476.6 9.1 collective-permute-start.1
  486.4 9.1 collective-permute-start.1
  496.2 9.1 collective-permute-start.1
  506.0 9.1 collective-permute-start.1
  515.8 9.1 collective-permute-start.1
  540.8 168.9 %reduce-scatter.10.cloned.1.call-start = ((), (), s32[]{:S(2)}) async-start(), calls=%async_computation.8 | async-start | bytes 884736
  567.2 13.9 %copy-start.26 = (f32[1,12,64,128]{3,2,1,0:T(8,128)S(1)}, f32[1,12,64,128]{3,2,1,0:T(8,128)}, u32[]{:S(2)}) copy-start(f32[1,12,64,128]{3,2,1,0:T(8,128)} %get-tuple-element.120) | copy-start | bytes 1179652
  567.2 13.9 %copy-start.29 = (f32[1,12,64,128]{3,2,1,0:T(8,128)S(1)}, f32[1,12,64,128]{3,2,1,0:T(8,128)}, u32[]{:S(2)}) copy-start(f32[1,12,64,128]{3,2,1,0:T(8,128)} %get-tuple-element.121) | copy-start | bytes 1179652
  634.1 14.2 %copy-start.8 = (bf16[1024,1536]{1,0:T(8,128)(2,1)S(1)}, bf16[1024,1536]{1,0:T(8,128)(2,1)}, u32[]{:S(2)}) copy-start(bf16[1024,1536]{1,0:T(8,128)(2,1)} %copy-done.7) | copy-start | bytes 9437188
  646.7 3.7 collective-permute-start.3
  650.3 175.3 %all-reduce.10.cloned.1.call-start = ((), (), s32[]{:S(2)}) async-start(), calls=%async_computation.9 | async-start | bytes 18874368
  658.0 9.9 copy-start.51
  682.8 368.1 %all-reduce.8.cloned.1.call-start = ((), (), s32[]{:S(2)}) async-start(), calls=%async_computation.5 | async-start | bytes 12582912 | tf_op jit(solution)/shard_map/psum | solution.py:240
  694.8 412.7 %reduce-scatter.8.cloned.1.call-start = ((), (), s32[]{:S(2)}) async-start(), calls=%async_computation.7 | async-start | bytes 5308416 | tf_op jit(solution)/shard_map/reduce_scatter | solution.py:254
  703.4 446.3 %reduce-scatter.6.cloned.1.call-start = ((), (), s32[]{:S(2)}) async-start(), calls=%async_computation.6 | async-start | bytes 1769472 | tf_op jit(solution)/shard_map/reduce_scatter | solution.py:252
  709.6 341.3 %copy-start.59 = (bf16[1536,256]{1,0:T(8,128)(2,1)S(1)}, bf16[1536,256]{1,0:T(8,128)(2,1)}, u32[]{:S(2)}) copy-start(bf16[1536,256]{1,0:T(8,128)(2,1)} %param.22) | copy-start | bytes 2359300
  709.6 341.3 %copy-start.67 = (f32[1536]{0:T(1024)S(1)}, f32[1536]{0:T(1024)}, u32[]{:S(2)}) copy-start(f32[1536]{0:T(1024)} %param.20) | copy-start | bytes 18436
  709.6 341.3 %copy-start.78 = (f32[1024]{0:T(1024)S(1)}, f32[1024]{0:T(1024)}, u32[]{:S(2)}) copy-start(f32[1024]{0:T(1024)} %copy-done.77) | copy-start | bytes 12292
  828.3 229.0 %copy-start.99 = (f32[768]{0:T(1024)S(1)}, f32[768]{0:T(1024)}, u32[]{:S(2)}) copy-start(f32[768]{0:T(1024)} %get-tuple-element.126) | copy-start | bytes 9220
  1082.7 67.0 %copy-start.1 = (bf16[1536,768]{1,0:T(8,128)(2,1)S(1)}, bf16[1536,768]{1,0:T(8,128)(2,1)}, u32[]{:S(2)}) copy-start(bf16[1536,768]{1,0:T(8,128)(2,1)} %param.30) | copy-start | bytes 7077892
  (91 other events, 360.5 us)
Sparse Core Ops, SparseCore 0:
  167.4 236.1 all-reduce.5
  540.8 90.6 all-gather.1
  650.5 34.1 reduce-scatter.9
  688.0 137.6 all-reduce.9
  827.9 222.9 all-reduce.7
  1054.7 52.7 reduce-scatter.7
  1111.3 38.3 reduce-scatter.5
